TPU v7x, 512 devices: a whole 4x4x16 slice. The times are simulated.
512 devices in a mesh: req: 64 (over x, z), tp: 8 (over y, core).
Axes of the slice: x: 4, y: 4, z: 16, core: 2. Of those that a mesh axis runs over, the one named last changes fastest.
Arguments:
- query_new: bfloat16 [8192, 2048], P('req', 'tp'), may hold values from -6 to 6
- key_new: bfloat16 [8192, 2048], P('req', 'tp'), may hold values from -6 to 6
- value_new: bfloat16 [8192, 2048], P('req', 'tp'), may hold values from -6 to 6
- mlp_hidden: bfloat16 [8192, 8192], P('req', 'tp'), may hold values from -6 to 6
- cache_pages: bfloat16 [4096, 16, 16, 256], P('req', None, 'tp'), may hold values from -6 to 6
- page_dest: int32 [4096, 1], P('req'), may hold values from 0 to 63; in each aligned block of 64 rows (0 to 63, 64 to 127, ...) at most 2 rows name the same one
- page_tag: int32 [4096], P('req'), may hold values from 0 to 3
- seg_ids: int32 [64, 128], P('req'), may hold values from 0 to 3, as said below
- attn_proj: bfloat16 [2048, 4096], P(('tp', 'req')), may hold values from -0.5 to 0.5
- mlp_down: bfloat16 [8192, 4096], P(('tp', 'req')), may hold values from -0.0625 to 0.0625
Outputs:
- layer_out: bfloat16 [8192, 4096], P('req', 'tp')
Inputs may be any that keep to these rules, and one draw needn't show every extreme that they name: `seg_ids`: within each pack the ids never fall; request 0 covers exactly the first 64 tokens and requests 1 to 3 each cover one or more of the rest. `page_dest`: among the rows of one device, at most 2 pages name the same destination, a bound that some block reaches.
All inputs are finite; a program needn't handle non-finite values.
Results may differ from a plain program's by a relative error of at most 0.014.
Values may be sent and summed in bfloat16 or wider, within the bound.
A program may use at most 128 MiB of HBM per device.

v0:
```python
import math
import jax
import jax.numpy as jnp
from jax import lax
from jax.sharding import PartitionSpec as P

HD = 128
ROT = 32
SEG_DEV = 4
CAP = 2


def rotate_heads(values, position, rot_dims):
    half_rot = rot_dims // 2
    frequency = 10000.0 ** (-2.0 * jnp.arange(half_rot, dtype=jnp.float32) / rot_dims)
    angles = position.astype(jnp.float32)[:, None] * frequency[None, :]
    cosine = jnp.cos(angles)[:, None, :]
    sine_part = jnp.sin(angles)[:, None, :]
    leading = values[..., :half_rot]
    trailing = values[..., half_rot:rot_dims]
    return jnp.concatenate(
        [
            leading * cosine - trailing * sine_part,
            trailing * cosine + leading * sine_part,
            values[..., rot_dims:],
        ],
        axis=-1,
    )


def masked_scores(query_rot, block_keys, segment, block_tags, score_scale):
    scores = (
        jnp.einsum("qhd,khd->hqk", query_rot, block_keys, preferred_element_type=jnp.float32)
        * score_scale
    )
    return jnp.where((segment[:, None] == block_tags[None, :])[None], scores, -jnp.inf)


def body(
    query_new,
    key_new,
    value_new,
    mlp_hidden,
    cache_pages,
    page_dest,
    page_tag,
    seg_ids,
    attn_proj,
    mlp_down,
):
    req_count = lax.axis_size("req")
    tok_count = query_new.shape[0]
    heads_local = query_new.shape[1] // HD
    page_rows = cache_pages.shape[1]
    pages_local = cache_pages.shape[0]
    slot_count = req_count * CAP
    score_scale = 1.0 / math.sqrt(HD)
    destination = page_dest[:, 0]
    dest_match = (destination[:, None] == jnp.arange(req_count, dtype=jnp.int32)[None, :]).astype(
        jnp.int32
    )
    earlier = jnp.cumsum(dest_match, axis=0) - dest_match
    rank = jnp.sum(earlier * dest_match, axis=1)
    slot_of_page = destination * CAP + rank
    select = jnp.arange(slot_count, dtype=jnp.int32)[:, None] == slot_of_page[None, :]
    flat_pages = cache_pages.reshape(pages_local, page_rows * heads_local * 2 * HD)
    send_pages = jnp.dot(
        select.astype(jnp.bfloat16), flat_pages, preferred_element_type=jnp.float32
    ).astype(jnp.bfloat16)
    send_pages = send_pages.reshape(req_count, CAP * page_rows, heads_local, 2 * HD)
    send_tags = (
        (jnp.sum(jnp.where(select, page_tag[None, :] + 1, 0), axis=1) - 1)
        .astype(jnp.bfloat16)
        .reshape(req_count, CAP)
    )
    recv_pages, recv_tags = (
        lax.all_to_all(send_pages, "req", split_axis=0, concat_axis=0, tiled=True),
        lax.all_to_all(send_tags, "req", split_axis=0, concat_axis=0, tiled=True),
    )
    slot_pages = recv_pages.reshape(slot_count, page_rows, heads_local, 2 * HD)
    slot_tags = recv_tags.reshape(slot_count).astype(jnp.int32)
    segment = seg_ids[0]
    seg_range = jnp.arange(SEG_DEV, dtype=jnp.int32)
    seg_first = jnp.sum((segment[:, None] < seg_range[None, :]).astype(jnp.int32), axis=0)
    prefix = page_rows * jnp.sum(
        (slot_tags[:, None] == seg_range[None, :]).astype(jnp.int32), axis=0
    )
    seg_match = segment[:, None] == seg_range[None, :]
    offset = jnp.sum(jnp.where(seg_match, prefix[None, :] - seg_first[None, :], 0), axis=1)
    row_index = jnp.arange(tok_count, dtype=jnp.int32)
    position = row_index + offset
    query_rot = rotate_heads(
        query_new.reshape(tok_count, heads_local, HD).astype(jnp.float32), position, ROT
    ).astype(jnp.bfloat16)
    key_rot = rotate_heads(
        key_new.reshape(tok_count, heads_local, HD).astype(jnp.float32), position, ROT
    ).astype(jnp.bfloat16)
    value_heads = value_new.reshape(tok_count, heads_local, HD)
    local_scores = (
        jnp.einsum("qhd,khd->hqk", query_rot, key_rot, preferred_element_type=jnp.float32)
        * score_scale
    )
    causal = (segment[:, None] == segment[None, :]) & (row_index[None, :] <= row_index[:, None])
    local_scores = jnp.where(causal[None], local_scores, -jnp.inf)
    cache_rows = slot_pages.reshape(slot_count * page_rows, heads_local, 2 * HD)
    key_tags = jnp.repeat(slot_tags, page_rows)
    cached = masked_scores(query_rot, cache_rows[..., :HD], segment, key_tags, score_scale)
    row_max = jnp.maximum(jnp.max(local_scores, axis=2), jnp.max(cached, axis=2))
    local_exp = jnp.exp(local_scores - row_max[..., None])
    cached_exp = jnp.exp(cached - row_max[..., None])
    denominator = jnp.sum(local_exp, axis=2) + jnp.sum(cached_exp, axis=2)
    local_weights = (local_exp / denominator[..., None]).astype(jnp.bfloat16)
    cached_weights = (cached_exp / denominator[..., None]).astype(jnp.bfloat16)
    attention = jnp.einsum(
        "hqk,khd->qhd", local_weights, value_heads, preferred_element_type=jnp.float32
    )
    attention = attention + jnp.einsum(
        "hqk,khd->qhd", cached_weights, cache_rows[..., HD:], preferred_element_type=jnp.float32
    )
    attn_flat = attention.astype(jnp.bfloat16).reshape(tok_count, heads_local * HD)
    columns = attn_flat
    attn_part = jnp.dot(
        columns,
        lax.all_gather(attn_proj, "req", axis=0, tiled=True),
        preferred_element_type=jnp.float32,
    )
    columns = mlp_hidden
    partial_value = attn_part + jnp.dot(
        columns,
        lax.all_gather(mlp_down, "req", axis=0, tiled=True),
        preferred_element_type=jnp.float32,
    )
    return lax.psum_scatter(
        partial_value.astype(jnp.bfloat16), "tp", scatter_dimension=1, tiled=True
    )


def solution(mesh):
    return jax.shard_map(
        body,
        mesh=mesh,
        in_specs=(
            P("req", "tp"),
            P("req", "tp"),
            P("req", "tp"),
            P("req", "tp"),
            P("req", None, "tp", None),
            P("req", None),
            P("req"),
            P("req", None),
            P(("tp", "req"), None),
            P(("tp", "req"), None),
        ),
        out_specs=P("req", "tp"),
        check_vma=False,
    )
```

profile of v0, /device:TPU:4, one launch (start us, length us, event | category | flops | bytes accessed | tf_op | source)
XLA Modules:
  0.0 378.9 jit_solution(5007309284389272083)
XLA Ops:
  6.5 0.0 copy-start
  6.5 0.0 all-gather.6.cloned.1.call-start
  6.5 0.7 all-gather.6.cloned.1.call-update
  7.3 0.0 all-gather.4.cloned.1.call-start
  7.3 0.7 all-gather.4.cloned.1.call-update
  8.0 0.7 fusion.17
  8.7 0.1 reduce_window_sum.11
  8.8 0.8 select_reduce_fusion.1
  9.7 0.7 multiply_add_fusion
  10.4 0.1 select_reduce_fusion
  10.5 0.8 convert_element_type.89
  11.3 18.7 %all-to-all-start = ((bf16[64,1,2]{2,1,0:T(2,128)(2,1)}), bf16[64,1,2]{2,1,0:T(2,128)(2,1)S(1)}, u32[]{:S(2)}, u32[]{:S(2)}) async-start(bf16[64,1,2]{2,1,0:T(2,128)(2,1)} %convert_element_type.89), calls=%async_computation | async-start | bytes 65536 | tf_op jit(solution)/shard_map/all_to_all | solution.py:78
  30.0 1.8 reshape.208
  31.8 0.8 convolution_convert_fusion
  32.6 2.8 reshape.209
  35.4 0.0 copy-start.2
  35.5 0.0 copy-start.3
  35.5 0.0 copy-start.4
  35.5 0.0 copy-start.5
  35.5 7.2 %all-to-all-done = bf16[64,1,2]{2,1,0:T(2,128)(2,1)S(1)} async-done(((bf16[64,1,2]{2,1,0:T(2,128)(2,1)}), bf16[64,1,2]{2,1,0:T(2,128)(2,1)S(1)}, u32[]{:S(2)}, u32[]{:S(2)}) %all-to-all-start) | async-done | bytes 288 | tf_op jit(solution)/shard_map/all_to_all | solution.py:78
  42.6 8.1 %all-to-all-start.1 = ((bf16[64,32,2,256]{3,2,1,0:T(2,128)(2,1)}), bf16[64,32,2,256]{3,2,1,0:T(2,128)(2,1)S(1)}, u32[]{:S(2)}, u32[]{:S(2)}) async-start(bf16[64,32,2,256]{3,2,1,0:T(2,128)(2,1)} %reshape.209), calls=%async_computation.1 | async-start | bytes 4194304 | tf_op jit(solution)/shard_map/all_to_all | solution.py:77
  50.8 0.0 reduce-scatter.2.cloned.1.call-start
  50.8 0.0 copy-done.2
  50.8 0.1 copy.47
  50.9 0.1 copy.48
  51.1 0.1 slice.36
  51.2 0.0 copy-done.3
  51.2 0.1 copy.53
  51.3 0.1 copy.54
  51.5 0.1 slice.39
  51.5 0.0 copy-done.4
  51.6 0.1 copy.62
  51.7 0.0 copy-done.5
  51.7 0.1 convert_reduce_fusion.1
  51.8 0.1 fusion.16
  51.9 0.1 convert_reduce_fusion
  52.0 0.1 reshape.212
  52.2 0.1 convert_reduce_fusion.2
  52.3 0.1 select_reduce_fusion.2
  52.4 0.1 multiply_cosine_fusion
  52.5 0.1 copy.51
  52.6 0.1 copy.50
  52.7 0.1 broadcast_in_dim.56
  52.8 0.1 eq.110
  52.9 0.1 subtract_convert_fusion
  53.0 0.3 fusion.20
  53.3 0.2 broadcast_compare_fusion
  53.5 121.6 %all-gather.6.cloned.1.call-done = bf16[64,4,4096]{2,1,0:T(4,128)(2,1)} async-done(((bf16[1,4,4096]{2,1,0:T(4,128)(2,1)}), bf16[64,4,4096]{2,1,0:T(4,128)(2,1)}) %all-gather.6.cloned.1.call-update) | async-done | bytes 2097168 | tf_op jit(solution)/shard_map/all_gather | solution.py:124
  175.1 4.0 %reshape.214 = bf16[256,4096]{1,0:T(8,128)(2,1)} reshape(bf16[64,4,4096]{2,1,0:T(4,128)(2,1)} %all-gather.6.cloned.1.call-done) | data formatting | bytes 4194304
  179.1 0.0 all-to-all-done.1
  179.1 0.4 copy.56
  179.6 0.7 fusion.21
  180.4 0.4 fusion.2
  180.8 0.8 convolution_bitcast_fusion.1
  181.6 0.2 fusion.5
  181.8 0.0 copy-start.1
  181.8 147.8 %all-gather.4.cloned.1.call-done = bf16[1024,4096]{1,0:T(8,128)(2,1)} async-done(((bf16[16,4096]{1,0:T(8,128)(2,1)}), bf16[1024,4096]{1,0:T(8,128)(2,1)}) %all-gather.4.cloned.1.call-update) | async-done | bytes 8388624 | tf_op jit(solution)/shard_map/all_gather | solution.py:130
  329.6 0.0 copy-done
  329.6 4.6 %fusion.22 = f32[128,4096]{1,0:T(8,128)S(1)} fusion(bf16[128,1024]{1,0:T(8,128)(2,1)S(1)} %copy-done, bf16[1024,4096]{1,0:T(8,128)(2,1)} %all-gather.4.cloned.1.call-done), kind=kOutput, calls=%fused_computation.58 | convolution fusion | flops 1073741824 | bytes 10747904 | tf_op jit(solution)/shard_map/dot_general | solution.py:128
  334.2 0.0 copy-done.1
  334.2 1.5 fusion
  335.7 0.0 reduce-scatter.2.cloned.1.call-update
  335.8 36.6 %reduce-scatter.2.cloned.1.call-done = bf16[128,512]{1,0:T(8,128)(2,1)} async-done(((bf16[128,4096]{1,0:T(8,128)(2,1)}), bf16[128,512]{1,0:T(8,128)(2,1)}) %reduce-scatter.2.cloned.1.call-update) | async-done | bytes 131088 | tf_op jit(solution)/shard_map/reduce_scatter | solution.py:133
  (9 shorter events, 0.1 us)
Async XLA Ops:
  6.5 323.0 %copy-start = (bf16[128,1024]{1,0:T(8,128)(2,1)S(1)}, bf16[128,1024]{1,0:T(8,128)(2,1)}, u32[]{:S(2)}) copy-start(bf16[128,1024]{1,0:T(8,128)(2,1)} %param.13) | copy-start | bytes 786436
  6.5 168.6 %all-gather.6.cloned.1.call-start = ((), (), s32[]{:S(2)}) async-start(), calls=%async_computation.5 | async-start | bytes 2129920 | tf_op jit(solution)/shard_map/all_gather | solution.py:124
  7.3 322.3 %all-gather.4.cloned.1.call-start = ((), (), s32[]{:S(2)}) async-start(), calls=%async_computation.3 | async-start | bytes 8519680 | tf_op jit(solution)/shard_map/all_gather | solution.py:130
  11.3 31.4 %all-to-all-start = ((bf16[64,1,2]{2,1,0:T(2,128)(2,1)}), bf16[64,1,2]{2,1,0:T(2,128)(2,1)S(1)}, u32[]{:S(2)}, u32[]{:S(2)}) async-start(bf16[64,1,2]{2,1,0:T(2,128)(2,1)} %convert_element_type.89), calls=%async_computation | async-start | bytes 65536 | tf_op jit(solution)/shard_map/all_to_all | solution.py:78
  35.4 15.4 %copy-start.2 = (bf16[128,256]{1,0:T(8,128)(2,1)S(1)}, bf16[128,256]{1,0:T(8,128)(2,1)}, u32[]{:S(2)}) copy-start(bf16[128,256]{1,0:T(8,128)(2,1)} %param.10) | copy-start | bytes 196612
  35.5 15.7 %copy-start.3 = (bf16[128,256]{1,0:T(8,128)(2,1)S(1)}, bf16[128,256]{1,0:T(8,128)(2,1)}, u32[]{:S(2)}) copy-start(bf16[128,256]{1,0:T(8,128)(2,1)} %param.11) | copy-start | bytes 196612
  35.5 16.1 %copy-start.4 = (bf16[128,256]{1,0:T(8,128)(2,1)S(1)}, bf16[128,256]{1,0:T(8,128)(2,1)}, u32[]{:S(2)}) copy-start(bf16[128,256]{1,0:T(8,128)(2,1)} %param.12) | copy-start | bytes 196612
  35.5 16.2 %copy-start.5 = (s32[1,128]{1,0:T(1,128)S(1)}, s32[1,128]{1,0:T(1,128)}, u32[]{:S(2)}) copy-start(s32[1,128]{1,0:T(1,128)} %param.17) | copy-start | bytes 1540
  42.6 136.5 %all-to-all-start.1 = ((bf16[64,32,2,256]{3,2,1,0:T(2,128)(2,1)}), bf16[64,32,2,256]{3,2,1,0:T(2,128)(2,1)S(1)}, u32[]{:S(2)}, u32[]{:S(2)}) async-start(bf16[64,32,2,256]{3,2,1,0:T(2,128)(2,1)} %reshape.209), calls=%async_computation.1 | async-start | bytes 4194304 | tf_op jit(solution)/shard_map/all_to_all | solution.py:77
  50.8 321.7 %reduce-scatter.2.cloned.1.call-start = ((), (), s32[]{:S(2)}) async-start(), calls=%async_computation.4 | async-start | bytes 1179648 | tf_op jit(solution)/shard_map/reduce_scatter | solution.py:133
  181.8 152.4 %copy-start.1 = (bf16[256,4096]{1,0:T(8,128)(2,1)S(1)}, bf16[256,4096]{1,0:T(8,128)(2,1)}, u32[]{:S(2)}) copy-start(bf16[256,4096]{1,0:T(8,128)(2,1)} %reshape.214) | copy-start | bytes 6291460
Sparse Core Ops, SparseCore 0:
  10.3 164.8 all-gather.5
  178.1 151.4 all-gather.3
  335.9 36.4 reduce-scatter.1
where the time goes:
time: 379 us
  waiting for transfers between devices  315 us (83%)
  starting transfers between devices  26.9 us (7%)
  between operations  13.3 us (4%)
  local copies, waits for them, and re-layouts  11.2 us (3%)
  matrix products  8.96 us (2%)
  other arithmetic  3.99 us (1%)
    all_gather x1, waiting for transfers between devices, body(): lax.all_gather(mlp_down, 'req', axis=0, tiled=True)  148 us
    all_gather x1, waiting for transfers between devices, body(): lax.all_gather(attn_proj, 'req', axis=0, tiled=True)  122 us
    reduce_scatter x1, waiting for transfers between devices, body(): lax.psum_scatter(partial_value.astype(jnp.bfloat16), 'tp', scatter_dimens...  36.6 us
    all_to_all x1, starting transfers between devices, body(): lax.all_to_all(send_tags, 'req', split_axis=0, concat_axis=0, tiled=True)  18.7 us
    all_to_all x1, starting transfers between devices, body(): lax.all_to_all(send_pages, 'req', split_axis=0, concat_axis=0, tiled=True)  8.11 us
  transfers between devices with their start and end apart: 5, of which 4 were waited for; matrix products, arithmetic and copies ran while one was open for 5% of the time, Pallas kernels for 0%

commit v1 on v0

--- a/solution.py
+++ b/solution.py
@@ -127,7 +127,10 @@
     columns = mlp_hidden
     partial_value = attn_part + jnp.dot(
         columns,
-        lax.all_gather(mlp_down, "req", axis=0, tiled=True),
+        jnp.concatenate(
+            lax.all_to_all(jnp.stack(lax.axis_size("req") * [mlp_down], axis=0), "req", 0, 0),
+            axis=0,
+        ),
         preferred_element_type=jnp.float32,
     )
     return lax.psum_scatter(

time: 379 us -> 587 us (1.55)
  the two profiles are of different devices: /device:TPU:4 before, /device:TPU:6 now
where the time goes in v1:
time: 587 us; the launch traced here: 586 us
  waiting for transfers between devices  412 us (70%)
  blocking collectives  106 us (18%)
  starting transfers between devices  26.5 us (5%)
  local copies, waits for them, and re-layouts  15.4 us (3%)
  between operations  13.6 us (2%)
  matrix products  9.06 us (2%)
    all_gather x1, waiting for transfers between devices, body(): lax.all_gather(attn_proj, 'req', axis=0, tiled=True)  197 us
    all_to_all x1, waiting for transfers between devices, body(): lax.all_to_all(jnp.stack(lax.axis_size('req') * [mlp_down], axis=0), 'req...  171 us
    all_to_all x1, blocking collectives, body(): lax.all_to_all(send_pages, 'req', split_axis=0, concat_axis=0, tiled=True)  106 us
    reduce_scatter x1, waiting for transfers between devices, body(): lax.psum_scatter(partial_value.astype(jnp.bfloat16), 'tp', scatter_dimens...  35.9 us
    all_to_all x1, starting transfers between devices, body(): lax.all_to_all(send_tags, 'req', split_axis=0, concat_axis=0, tiled=True)  18.8 us
  transfers between devices with their start and end apart: 4, of which 4 were waited for; matrix products, arithmetic and copies ran while one was open for 2% of the time, Pallas kernels for 0%

profile of v1, /device:TPU:6, one launch (start us, length us, event | category | flops | bytes accessed | tf_op | source)
XLA Modules:
  0.0 586.1 jit_solution(15640518928090655160)
XLA Ops:
  6.5 0.0 copy-start
  6.5 0.8 fusion.17
  7.3 0.1 reduce_window_sum.11
  7.4 0.8 select_reduce_fusion.1
  8.2 0.7 multiply_add_fusion
  8.9 0.1 select_reduce_fusion
  9.0 0.8 convert_element_type.89
  9.8 18.8 %all-to-all-start = ((bf16[64,1,2]{2,1,0:T(2,128)(2,1)}), bf16[64,1,2]{2,1,0:T(2,128)(2,1)S(1)}, u32[]{:S(2)}, u32[]{:S(2)}) async-start(bf16[64,1,2]{2,1,0:T(2,128)(2,1)} %convert_element_type.89), calls=%async_computation | async-start | bytes 65536 | tf_op jit(solution)/shard_map/all_to_all | solution.py:78
  28.6 1.8 reshape.213
  30.5 0.8 convolution_convert_fusion
  31.3 2.8 reshape.214
  34.1 0.0 copy-start.2
  34.1 7.1 %all-to-all-done = bf16[64,1,2]{2,1,0:T(2,128)(2,1)S(1)} async-done(((bf16[64,1,2]{2,1,0:T(2,128)(2,1)}), bf16[64,1,2]{2,1,0:T(2,128)(2,1)S(1)}, u32[]{:S(2)}, u32[]{:S(2)}) %all-to-all-start) | async-done | bytes 288 | tf_op jit(solution)/shard_map/all_to_all | solution.py:78
  41.1 105.9 %all_to_all.16 = bf16[64,32,2,256]{3,2,1,0:T(2,128)(2,1)S(1)} all-to-all(bf16[64,32,2,256]{3,2,1,0:T(2,128)(2,1)} %reshape.214), channel_id=1, replica_groups=mesh['req'=64,'tp'=8] {'req'}, dimensions={0} | all-to-all | bytes 4194304 | tf_op jit(solution)/shard_map/all_to_all | solution.py:77
  147.0 0.0 copy-done.2
  147.0 4.3 stack.2
  151.3 0.0 copy-start.3
  151.3 0.0 copy-start.4
  151.3 0.0 copy-start.5
  151.3 0.0 copy-start.6
  151.3 7.7 %all-to-all-start.2 = ((bf16[64,16,4096]{2,1,0:T(8,128)(2,1)}), bf16[64,16,4096]{2,1,0:T(8,128)(2,1)}, u32[]{:S(2)}, u32[]{:S(2)}) async-start(bf16[64,16,4096]{2,1,0:T(8,128)(2,1)} %stack.2), calls=%async_computation.2 | async-start | bytes 16777216 | tf_op jit(solution)/shard_map/all_to_all | solution.py:131
  159.0 0.0 all-gather.3.cloned.1.call-start
  159.0 0.7 all-gather.3.cloned.1.call-update
  159.7 0.0 reduce-scatter.2.cloned.1.call-start
  159.8 0.0 copy-done.3
  159.8 0.1 copy.47
  159.9 0.1 copy.48
  160.0 0.1 slice.36
  160.2 0.0 copy-done.4
  160.2 0.1 copy.53
  160.3 0.1 copy.54
  160.4 0.1 slice.39
  160.5 0.0 copy-done.5
  160.5 0.1 copy.62
  160.7 0.0 copy-done.6
  160.7 0.1 convert_reduce_fusion.1
  160.8 0.1 fusion.16
  160.9 0.1 convert_reduce_fusion
  161.0 0.1 reshape.218
  161.1 0.1 convert_reduce_fusion.2
  161.3 0.1 select_reduce_fusion.2
  161.4 0.1 multiply_cosine_fusion
  161.5 0.1 copy.51
  161.6 0.1 copy.50
  161.7 0.1 broadcast_in_dim.56
  161.8 0.1 eq.110
  161.9 0.1 subtract_convert_fusion
  162.0 0.3 fusion.20
  162.3 0.2 broadcast_compare_fusion
  162.5 197.2 %all-gather.3.cloned.1.call-done = bf16[64,4,4096]{2,1,0:T(4,128)(2,1)} async-done(((bf16[1,4,4096]{2,1,0:T(4,128)(2,1)}), bf16[64,4,4096]{2,1,0:T(4,128)(2,1)}) %all-gather.3.cloned.1.call-update) | async-done | bytes 2097168 | tf_op jit(solution)/shard_map/all_gather | solution.py:124
  359.8 4.0 reshape.220
  363.7 0.4 copy.56
  364.2 0.7 fusion.21
  365.0 0.4 fusion.2
  365.4 0.8 convolution_bitcast_fusion.1
  366.2 0.2 fusion.5
  366.4 170.7 %all-to-all-done.2 = bf16[64,16,4096]{2,1,0:T(8,128)(2,1)} async-done(((bf16[64,16,4096]{2,1,0:T(8,128)(2,1)}), bf16[64,16,4096]{2,1,0:T(8,128)(2,1)}, u32[]{:S(2)}, u32[]{:S(2)}) %all-to-all-start.2) | async-done | bytes 8388640 | tf_op jit(solution)/shard_map/all_to_all | solution.py:131
  537.1 0.0 copy-done
  537.1 0.0 copy-start.1
  537.1 4.8 fusion.22
  541.9 0.0 copy-done.1
  541.9 1.5 fusion
  543.4 0.0 reduce-scatter.2.cloned.1.call-update
  543.4 35.9 %reduce-scatter.2.cloned.1.call-done = bf16[128,512]{1,0:T(8,128)(2,1)} async-done(((bf16[128,4096]{1,0:T(8,128)(2,1)}), bf16[128,512]{1,0:T(8,128)(2,1)}) %reduce-scatter.2.cloned.1.call-update) | async-done | bytes 131088 | tf_op jit(solution)/shard_map/reduce_scatter | solution.py:136
  (9 shorter events, 0.1 us)
Async XLA Ops:
  6.5 530.6 %copy-start = (bf16[128,1024]{1,0:T(8,128)(2,1)S(1)}, bf16[128,1024]{1,0:T(8,128)(2,1)}, u32[]{:S(2)}) copy-start(bf16[128,1024]{1,0:T(8,128)(2,1)} %param.13) | copy-start | bytes 786436
  9.8 31.3 %all-to-all-start = ((bf16[64,1,2]{2,1,0:T(2,128)(2,1)}), bf16[64,1,2]{2,1,0:T(2,128)(2,1)S(1)}, u32[]{:S(2)}, u32[]{:S(2)}) async-start(bf16[64,1,2]{2,1,0:T(2,128)(2,1)} %convert_element_type.89), calls=%async_computation | async-start | bytes 65536 | tf_op jit(solution)/shard_map/all_to_all | solution.py:78
  34.1 113.0 %copy-start.2 = (bf16[16,4096]{1,0:T(8,128)(2,1)S(1)}, bf16[16,4096]{1,0:T(8,128)(2,1)}, u32[]{:S(2)}) copy-start(bf16[16,4096]{1,0:T(8,128)(2,1)} %param.19) | copy-start | bytes 393220
  151.3 8.5 %copy-start.3 = (bf16[128,256]{1,0:T(8,128)(2,1)S(1)}, bf16[128,256]{1,0:T(8,128)(2,1)}, u32[]{:S(2)}) copy-start(bf16[128,256]{1,0:T(8,128)(2,1)} %param.10) | copy-start | bytes 196612
  151.3 8.9 %copy-start.4 = (bf16[128,256]{1,0:T(8,128)(2,1)S(1)}, bf16[128,256]{1,0:T(8,128)(2,1)}, u32[]{:S(2)}) copy-start(bf16[128,256]{1,0:T(8,128)(2,1)} %param.11) | copy-start | bytes 196612
  151.3 9.2 %copy-start.5 = (bf16[128,256]{1,0:T(8,128)(2,1)S(1)}, bf16[128,256]{1,0:T(8,128)(2,1)}, u32[]{:S(2)}) copy-start(bf16[128,256]{1,0:T(8,128)(2,1)} %param.12) | copy-start | bytes 196612
  151.3 9.4 %copy-start.6 = (s32[1,128]{1,0:T(1,128)S(1)}, s32[1,128]{1,0:T(1,128)}, u32[]{:S(2)}) copy-start(s32[1,128]{1,0:T(1,128)} %param.17) | copy-start | bytes 1540
  151.3 385.8 %all-to-all-start.2 = ((bf16[64,16,4096]{2,1,0:T(8,128)(2,1)}), bf16[64,16,4096]{2,1,0:T(8,128)(2,1)}, u32[]{:S(2)}, u32[]{:S(2)}) async-start(bf16[64,16,4096]{2,1,0:T(8,128)(2,1)} %stack.2), calls=%async_computation.2 | async-start | bytes 16777216 | tf_op jit(solution)/shard_map/all_to_all | solution.py:131
  159.0 200.8 %all-gather.3.cloned.1.call-start = ((), (), s32[]{:S(2)}) async-start(), calls=%async_computation.5 | async-start | bytes 2129920 | tf_op jit(solution)/shard_map/all_gather | solution.py:124
  159.7 419.6 %reduce-scatter.2.cloned.1.call-start = ((), (), s32[]{:S(2)}) async-start(), calls=%async_computation.4 | async-start | bytes 1179648 | tf_op jit(solution)/shard_map/reduce_scatter | solution.py:136
  537.1 4.8 copy-start.1
Sparse Core Ops, SparseCore 0:
  162.8 196.9 all-gather.2
  543.5 35.7 reduce-scatter.1
